TPU v7x, 512 devices: a whole 4x4x16 slice. The times are simulated.
512 devices in a mesh: sub: 64 (over x, z), grp: 8 (over y, core).
Axes of the slice: x: 4, y: 4, z: 16, core: 2. Of those that a mesh axis runs over, the one named last changes fastest.
Arguments:
- rhs_jump: float32 [64, 8, 256, 256], P('sub', 'grp'), may hold values from -6 to 6
- incision: int32 [64, 8, 256], P('sub', 'grp'), may hold values 0 or 1
- precond: float32 [64, 8, 256], P('sub', 'grp'), may hold values from 0.5 to 2
- left_rows: int32 [64, 8, 256], P('sub', 'grp'), may hold values from 0 to 1151, as said below
- right_rows: int32 [64, 8, 256], P('sub', 'grp'), may hold values from 0 to 1151, as said below
- diag_inv: float32 [64, 8, 3, 384, 384], P('sub', 'grp'), as said below
- coupling: float32 [64, 8, 2, 384, 384], P('sub', 'grp'), may hold values from -0.09185587 to 0.09185587
- coarse_basis: float32 [64, 8, 3, 384, 128], P('sub', 'grp'), may hold values from -0.25 to 0.25
- coarse_inv: float32 [64, 128, 128], P('sub'), as said below
Outputs:
- multipliers: float32 [64, 8, 256, 256], P('sub', 'grp')
- residual: float32 [64, 8, 256, 256], P('sub', 'grp')
Inputs may be any that keep to these rules, and one draw needn't show every extreme that they name: `left_rows`: for each subdomain, its 256 left rows and 256 right rows are 512 distinct interior rows. `right_rows`: see left_rows. `diag_inv`: every block is invertible. `coarse_inv`: every block is symmetric positive definite.
All inputs are finite; a program needn't handle non-finite values. No bound on the sum of `incision` on one device may be relied on, other than what follows from the above.
Results may differ from a plain program's by a relative error of at most 0.0003.
Values sent between devices are 32-bit elements; how exact they have to be, the bound alone decides.
No kernel may reach another device: no remote copies, remote signals or barrier semaphores. Data moves between devices by JAX's collectives and lax.ppermute only.
A program may use at most 64 MiB of HBM per device.

v0:
```python
import jax
import jax.numpy as jnp
from jax import lax
from jax.sharding import PartitionSpec as P

ITERS = 3
HIGH = lax.Precision.HIGHEST


def passed_along(shard, axis, by):
    peers = lax.axis_size(axis)
    return lax.ppermute(shard, axis, [(i, (i + by) % peers) for i in range(peers)])


def norm_total(value):
    return lax.psum(value, ("sub", "grp"))


def local(
    rhs_jump, incision, precond, left_rows, right_rows, diag_inv, coupling, coarse_basis, coarse_inv
):
    load_rhs = rhs_jump[0, 0]
    cut = incision[0, 0].astype(jnp.float32)[:, None]
    scaling = precond[0, 0][:, None]
    lrow = left_rows[0, 0]
    rrow = right_rows[0, 0]
    dinv = diag_inv[0, 0]
    coup = coupling[0, 0]
    nblk, blk = (dinv.shape[0], dinv.shape[1])
    order = nblk * blk
    basis = coarse_basis[0, 0].reshape(order, -1)
    cinv = coarse_inv[0]
    width = load_rhs.shape[1]
    start = load_rhs[None]
    scales = scaling[None]
    cuts = cut[None]

    def local_dot(first, second):
        return jnp.sum(first[-1] * second[-1], axis=0)

    multipliers = jnp.zeros_like(start)
    residual = cuts * start
    zvec = scales * residual
    direc = zvec
    rz_now = norm_total(local_dot(residual, zvec))
    for step in range(ITERS):
        apply_own = direc[0]
        apply_left = passed_along(apply_own, "sub", 1)
        zeros = jnp.zeros((order, width), jnp.float32)
        interior_load = zeros.at[rrow].add(apply_own).at[lrow].add(-apply_left)
        primal = jnp.einsum("np,nr->pr", basis, interior_load, precision=HIGH)
        summed = lax.psum(primal, "grp")
        pieces = interior_load.reshape(nblk, blk, width)
        forward = []
        for block in range(nblk):
            rhs_now = pieces[block]
            if block > 0:
                rhs_now = rhs_now - jnp.dot(coup[block - 1], forward[-1], precision=HIGH)
            forward.append(jnp.dot(dinv[block], rhs_now, precision=HIGH))
        backward = [None] * nblk
        for block in range(nblk - 1, -1, -1):
            rhs_now = forward[block]
            if block < nblk - 1:
                rhs_now = rhs_now - jnp.dot(coup[block].T, backward[block + 1], precision=HIGH)
            backward[block] = jnp.dot(dinv[block].T, rhs_now, precision=HIGH)
        solved = jnp.concatenate(backward, axis=0)
        coarse = jnp.dot(cinv, summed, precision=HIGH)
        disp = solved + jnp.dot(basis, coarse, precision=HIGH)
        yleft = jnp.take(disp, lrow, axis=0)
        yright = jnp.take(disp, rrow, axis=0)
        nextone = passed_along(yleft, "sub", -1)
        image = (cut * (yright - nextone))[None]
        alpha = rz_now / lax.psum(local_dot(direc, image), ("sub", "grp"))
        multipliers = multipliers + alpha * direc
        residual = residual - alpha * image
        if step + 1 < ITERS:
            zvec = scales * residual
            rz_new = norm_total(local_dot(residual, zvec))
            direc = zvec + rz_new / rz_now * direc
            rz_now = rz_new
    return (multipliers[-1][None, None], residual[-1][None, None])


def solution(mesh):
    placed = (
        P("sub", "grp", None, None),
        P("sub", "grp", None),
        P("sub", "grp", None),
        P("sub", "grp", None),
        P("sub", "grp", None),
        P("sub", "grp", None, None, None),
        P("sub", "grp", None, None, None),
        P("sub", "grp", None, None, None),
        P("sub", None, None),
    )
    return jax.shard_map(
        local,
        mesh=mesh,
        in_specs=placed,
        out_specs=(P("sub", "grp", None, None), P("sub", "grp", None, None)),
        check_vma=False,
    )
```

profile of v0, /device:TPU:1, one launch (start us, length us, event | category | flops | bytes accessed | tf_op | source)
XLA Modules:
  0.0 924.1 jit_solution(12377833747426889409)
XLA Ops:
  9.1 4.4 collective-permute-start
  16.2 3.6 scatter_custom_fusion
  20.4 8.8 collective-permute-done
  29.9 4.7 scatter_custom_fusion.1
  34.7 2.5 fusion.46
  38.0 1.5 fusion.31
  40.3 1.5 fusion.13
  44.5 1.6 convolution_subtract_fusion.4
  46.2 2.7 convolution_bitcast_fusion.14
  49.2 2.7 convolution_bitcast_fusion.9
  51.8 67.6 %all-reduce.5.cloned.1.call-done = f32[128,256]{0,1:T(8,128)} async-done(((f32[128,256]{0,1:T(8,128)}), f32[128,256]{0,1:T(8,128)}) %all-reduce.5.cloned.1.call-update) | async-done | bytes 131088 | tf_op jit(solution)/shard_map/psum | solution.py:52
  119.4 1.2 fusion.103
  120.6 3.3 fusion.2
  123.9 2.7 copy.17
  126.6 2.9 gather_fusion.1
  129.5 1.8 broadcast_select_fusion.2
  131.3 7.0 collective-permute-start.1
  139.7 2.9 gather_fusion
  142.6 1.9 multiply_reduce_fusion.2
  144.5 106.5 %all-reduce = (f32[256]{0:T(256)}, f32[256]{0:T(256)}) all-reduce(f32[256]{0:T(256)} %get-tuple-element.4, f32[256]{0:T(256)S(1)} %get-tuple-element.3), channel_id=1, replica_groups=mesh['sub'=64,'grp'=8] {'sub','grp'}, use_global_device_ids=true, to_apply=%region_1.0 | all-reduce | flops 512 | bytes 4096 | tf_op jit(solution)/shard_map/psum | solution.py:16
  251.7 2.6 fusion.87
  254.2 98.8 %psum.66 = f32[256]{0:T(256)S(1)} all-reduce(f32[256]{0:T(256)} %get-tuple-element.9), channel_id=1, replica_groups=mesh['sub'=64,'grp'=8] {'sub','grp'}, use_global_device_ids=true, to_apply=%region_8.10 | all-reduce | flops 256 | bytes 2048 | tf_op jit(solution)/shard_map/psum | solution.py:16
  353.7 1.9 multiply_add_fusion.1
  355.5 3.7 collective-permute-start.2
  359.2 3.4 scatter_custom_fusion.2
  362.6 5.6 collective-permute-done.2
  368.3 4.9 scatter_custom_fusion.3
  373.1 3.3 fusion.43
  376.4 2.7 convolution_bitcast_fusion.13
  379.1 1.9 convolution_bitcast_fusion.8
  381.0 1.5 fusion.27
  383.3 1.5 fusion.9
  388.3 1.7 convolution_subtract_fusion.2
  390.2 2.6 convolution_bitcast_fusion.6
  392.8 62.3 %all-reduce.7.cloned.1.call-done = f32[128,256]{0,1:T(8,128)} async-done(((f32[128,256]{0,1:T(8,128)}), f32[128,256]{0,1:T(8,128)}) %all-reduce.7.cloned.1.call-update) | async-done | bytes 131088 | tf_op jit(solution)/shard_map/psum | solution.py:52
  455.2 1.2 fusion.101
  456.4 3.4 fusion.1
  459.7 2.6 copy.19
  462.4 3.0 gather_fusion.3
  465.4 1.7 broadcast_select_fusion.1
  467.2 7.0 collective-permute-start.3
  474.2 3.1 gather_fusion.2
  477.8 1.8 multiply_reduce_fusion.1
  479.6 107.2 %psum.68 = f32[256]{0:T(256)} all-reduce(f32[256]{0:T(256)} %multiply_reduce_fusion.1), channel_id=1, replica_groups=mesh['sub'=64,'grp'=8] {'sub','grp'}, use_global_device_ids=true, to_apply=%region_13.15 | all-reduce | flops 256 | bytes 2048 | tf_op jit(solution)/shard_map/psum | solution.py:73
  588.0 2.6 fusion.88
  590.6 98.5 %psum.69 = f32[256]{0:T(256)} all-reduce(f32[256]{0:T(256)} %get-tuple-element.7), channel_id=1, replica_groups=mesh['sub'=64,'grp'=8] {'sub','grp'}, use_global_device_ids=true, to_apply=%region_15.17 | all-reduce | flops 256 | bytes 2048 | tf_op jit(solution)/shard_map/psum | solution.py:16
  689.8 1.8 multiply_add_fusion
  691.6 3.7 collective-permute-start.4
  695.3 3.4 scatter_custom_fusion.4
  698.7 5.7 collective-permute-done.4
  704.3 4.7 scatter_custom_fusion.5
  709.0 3.3 fusion.40
  712.3 2.7 convolution_bitcast_fusion.12
  715.0 1.9 convolution_bitcast_fusion.5
  716.9 1.5 fusion.23
  719.2 1.5 fusion.5
  724.1 1.7 convolution_subtract_fusion
  725.9 3.0 convolution_bitcast_fusion.3
  728.8 62.6 %all-reduce.9.cloned.1.call-done = f32[128,256]{0,1:T(8,128)} async-done(((f32[128,256]{0,1:T(8,128)}), f32[128,256]{0,1:T(8,128)}) %all-reduce.9.cloned.1.call-update) | async-done | bytes 131088 | tf_op jit(solution)/shard_map/psum | solution.py:52
  792.6 2.2 fusion
  796.5 7.1 collective-permute-start.5
  804.7 2.2 collective-permute-done.5
  808.0 107.2 %psum.71 = f32[256]{0:T(256)S(1)} all-reduce(f32[256]{0:T(256)S(1)} %multiply_reduce_fusion), channel_id=1, replica_groups=mesh['sub'=64,'grp'=8] {'sub','grp'}, use_global_device_ids=true, to_apply=%region_20.22 | all-reduce | flops 256 | bytes 2048 | tf_op jit(solution)/shard_map/psum | solution.py:73
  915.3 2.0 subtract_bitcast_fusion
  (110 shorter events, 29.4 us)
Async XLA Ops:
  7.2 39.0 %copy-start = (f32[1,1,3,384,128]{4,3,2,1,0:T(8,128)S(1)}, f32[1,1,3,384,128]{4,3,2,1,0:T(8,128)}, u32[]{:S(2)}) copy-start(f32[1,1,3,384,128]{4,3,2,1,0:T(8,128)} %param.18) | copy-start | bytes 1769476
  7.2 12.7 %copy-start.31 = (s32[1,1,256]{2,1,0:T(1,128)S(1)}, s32[1,1,256]{2,1,0:T(1,128)}, u32[]{:S(2)}) copy-start(s32[1,1,256]{2,1,0:T(1,128)} %param.15) | copy-start | bytes 3076
  7.2 112.2 %all-reduce.5.cloned.1.call-start = ((), (), s32[]{:S(2)}) async-start(), calls=%async_computation | async-start | bytes 262144 | tf_op jit(solution)/shard_map/psum | solution.py:52
  9.1 20.1 %collective-permute-start = (f32[256,256]{1,0:T(8,128)S(1)}, f32[256,256]{1,0:T(8,128)S(1)}, u32[]{:S(2)}, u32[]{:S(2)}) collective-permute-start(f32[256,256]{1,0:T(8,128)S(1)} %fusion.98), channel_id=1, source_target_pairs={{0,8},{8,16},{16,24},{24,32},{32,40},{40,48},{48,56},{56,64},{64,7... | collective-permute-start | bytes 786440 | tf_op jit(solution)/shard_map/ppermute | solution.py:12
  14.1 20.5 %copy-start.32 = (s32[256,1]{0,1:T(1,128)}, s32[256,1]{0,1:T(1,128)S(1)}, u32[]{:S(2)}) copy-start(s32[256,1]{0,1:T(1,128)S(1)} %compare_select_fusion) | copy-start | bytes 3076
  15.5 114.1 %copy-start.29 = (pred[256]{0:T(512)(128)(4,1)}, pred[256]{0:T(512)(128)(4,1)S(1)}, u32[]{:S(2)}) copy-start(pred[256]{0:T(512)(128)(4,1)S(1)} %compare_and_fusion) | copy-start | bytes 772
  16.2 13.0 %copy-start.33 = (s32[256,1]{0,1:T(1,128)}, s32[256,1]{0,1:T(1,128)S(1)}, u32[]{:S(2)}) copy-start(s32[256,1]{0,1:T(1,128)S(1)} %compare_select_fusion.1) | copy-start | bytes 3076
  16.2 110.4 %copy-start.22 = (s32[1024]{0:T(1024)}, s32[1024]{0:T(1024)S(1)}, u32[]{:S(2)}) copy-start(s32[1024]{0:T(1024)S(1)} %pad_clamp_fusion) | copy-start | bytes 12292
  16.2 18.4 %copy-start.1 = (f32[1,1,3,384,384]{4,3,2,1,0:T(8,128)S(1)}, f32[1,1,3,384,384]{4,3,2,1,0:T(8,128)}, u32[]{:S(2)}) copy-start(f32[1,1,3,384,384]{4,3,2,1,0:T(8,128)} %param.16) | copy-start | bytes 5308420
  29.2 0.7 copy-start.20
  29.9 7.3 copy-start.2
  34.6 3.4 copy-start.7
  42.7 1.8 copy-start.9
  44.5 1.7 copy-start.10
  48.9 406.3 %all-reduce.7.cloned.1.call-start = ((), (), s32[]{:S(2)}) async-start(), calls=%async_computation.1 | async-start | bytes 262144 | tf_op jit(solution)/shard_map/psum | solution.py:52
  131.3 11.3 %collective-permute-start.1 = (f32[256,256]{1,0:T(8,128)}, f32[256,256]{1,0:T(8,128)}, u32[]{:S(2)}, u32[]{:S(2)}) collective-permute-start(f32[256,256]{1,0:T(8,128)} %broadcast_select_fusion.2), channel_id=1, source_target_pairs={{0,504},{8,0},{16,8},{24,16},{32,24},{40,32},{48,40},{56,48},{64,5... | collective-permute-start | bytes 786440 | tf_op jit(solution)/shard_map/ppermute | solution.py:12
  139.0 3.6 copy-start.23
  139.7 3.0 copy-start.21
  251.7 2.6 copy-start.25
  355.5 12.7 %collective-permute-start.2 = (f32[256,256]{1,0:T(8,128)}, f32[256,256]{1,0:T(8,128)}, u32[]{:S(2)}, u32[]{:S(2)}) collective-permute-start(f32[256,256]{1,0:T(8,128)} %multiply_add_fusion.1), channel_id=1, source_target_pairs={{0,8},{8,16},{16,24},{24,32},{32,40},{40,48},{48,56},{56,64},{64,7... | collective-permute-start | bytes 786440 | tf_op jit(solution)/shard_map/ppermute | solution.py:12
  373.1 3.3 copy-start.5
  379.1 1.9 copy-start.6
  385.7 1.8 copy-start.11
  385.7 2.6 copy-start.16
  387.5 0.7 copy-start.14
  390.0 401.5 %all-reduce.9.cloned.1.call-start = ((), (), s32[]{:S(2)}) async-start(), calls=%async_computation.2 | async-start | bytes 262144 | tf_op jit(solution)/shard_map/psum | solution.py:52
  467.2 10.6 %collective-permute-start.3 = (f32[256,256]{1,0:T(8,128)}, f32[256,256]{1,0:T(8,128)}, u32[]{:S(2)}, u32[]{:S(2)}) collective-permute-start(f32[256,256]{1,0:T(8,128)} %broadcast_select_fusion.1), channel_id=1, source_target_pairs={{0,504},{8,0},{16,8},{24,16},{32,24},{40,32},{48,40},{56,48},{64,5... | collective-permute-start | bytes 786440 | tf_op jit(solution)/shard_map/ppermute | solution.py:12
  587.4 0.6 copy-start.27
  691.6 12.7 %collective-permute-start.4 = (f32[256,256]{1,0:T(8,128)}, f32[256,256]{1,0:T(8,128)}, u32[]{:S(2)}, u32[]{:S(2)}) collective-permute-start(f32[256,256]{1,0:T(8,128)} %multiply_add_fusion), channel_id=1, source_target_pairs={{0,8},{8,16},{16,24},{24,32},{32,40},{40,48},{48,56},{56,64},{64,7... | collective-permute-start | bytes 786440 | tf_op jit(solution)/shard_map/ppermute | solution.py:12
  709.0 3.3 copy-start.3
  715.0 1.9 copy-start.4
  721.5 1.8 copy-start.12
  721.6 2.6 copy-start.17
  723.4 0.7 copy-start.15
  725.8 65.6 %copy-start.19 = (f32[1,128,128]{2,1,0:T(8,128)S(1)}, f32[1,128,128]{2,1,0:T(8,128)}, u32[]{:S(2)}) copy-start(f32[1,128,128]{2,1,0:T(8,128)} %param.19) | copy-start | bytes 196612
  725.8 66.8 %copy-start.13 = (f32[256,384]{1,0:T(8,128)S(1)}, f32[256,384]{1,0:T(8,128)}, u32[]{:S(2)}) copy-start(f32[256,384]{1,0:T(8,128)} %copy-done.12) | copy-start | bytes 1179652
  795.2 1.1 copy-start.30
  796.4 118.8 %copy-start.24 = (f32[256]{0:T(256)S(1)}, f32[256]{0:T(256)}, u32[]{:S(2)}) copy-start(f32[256]{0:T(256)} %psum.69) | copy-start | bytes 3076
  796.4 118.8 %copy-start.8 = (f32[1,1,256,256]{3,2,1,0:T(8,128)S(1)}, f32[1,1,256,256]{3,2,1,0:T(8,128)}, u32[]{:S(2)}) copy-start(f32[1,1,256,256]{3,2,1,0:T(8,128)} %param.11) | copy-start | bytes 786436
  796.5 118.8 %copy-start.18 = (f32[256,256]{1,0:T(8,128)S(1)}, f32[256,256]{1,0:T(8,128)}, u32[]{:S(2)}) copy-start(f32[256,256]{1,0:T(8,128)} %get-tuple-element.8) | copy-start | bytes 786436
  796.5 118.8 %copy-start.26 = (f32[256]{0:T(256)S(1)}, f32[256]{0:T(256)}, u32[]{:S(2)}) copy-start(f32[256]{0:T(256)} %copy-done.25) | copy-start | bytes 3076
  796.5 118.8 %copy-start.28 = (f32[256]{0:T(256)S(1)}, f32[256]{0:T(256)}, u32[]{:S(2)}) copy-start(f32[256]{0:T(256)} %copy-done.27) | copy-start | bytes 3076
  796.5 10.4 %collective-permute-start.5 = (f32[256,256]{1,0:T(8,128)S(1)}, f32[256,256]{1,0:T(8,128)S(1)}, u32[]{:S(2)}, u32[]{:S(2)}) collective-permute-start(f32[256,256]{1,0:T(8,128)S(1)} %broadcast_select_fusion), channel_id=1, source_target_pairs={{0,504},{8,0},{16,8},{24,16},{32,24},{40,32},{48,40},{56,48},{64,5... | collective-permute-start | bytes 786440 | tf_op jit(solution)/shard_map/ppermute | solution.py:12
Sparse Core Ops, SparseCore 0:
  49.0 70.3 all-reduce.4
  390.1 65.0 all-reduce.6
  726.0 65.3 all-reduce.8
where the time goes:
time: 929 us; the launch traced here: 924 us
  blocking collectives  518 us (56%)
  waiting for transfers between devices  215 us (23%)
  matrix products  66.8 us (7%)
  other arithmetic  53 us (6%)
  starting transfers between devices  33.3 us (4%)
  local copies, waits for them, and re-layouts  22.8 us (2%)
  between operations  14.6 us (2%)
    psum x3, blocking collectives, norm_total(): return lax.psum(value, ('sub', 'grp'))  304 us
    psum x2, blocking collectives, local(): alpha = rz_now / lax.psum(local_dot(direc, image), ('sub', 'grp'))  214 us
    psum x3, waiting for transfers between devices, local(): summed = lax.psum(primal, 'grp')  192 us
    ppermute x6, starting transfers between devices, passed_along(): lax.ppermute(shard, axis, [(i, (i + by) % peers) for i in range(peers)])  32.8 us
    scatter-add x6, other arithmetic, local(): interior_load = zeros.at[rrow].add(apply_own).at[lrow].add(-apply_left)  24.6 us
    ppermute x6, waiting for transfers between devices, passed_along(): lax.ppermute(shard, axis, [(i, (i + by) % peers) for i in range(peers)])  22.8 us
  transfers between devices with their start and end apart: 9, of which 8 were waited for; matrix products, arithmetic and copies ran while one was open for 3% of the time, Pallas kernels for 0%

commit v1 on v0

--- a/solution.py
+++ b/solution.py
@@ -5,6 +5,11 @@
 
 ITERS = 3
 HIGH = lax.Precision.HIGHEST
+
+
+def one_after_other(value_2, one, other):
+    inner = lax.psum(value_2, one)
+    return lax.psum(inner, other)
 
 
 def passed_along(shard, axis, by):
@@ -70,7 +75,7 @@
         yright = jnp.take(disp, rrow, axis=0)
         nextone = passed_along(yleft, "sub", -1)
         image = (cut * (yright - nextone))[None]
-        alpha = rz_now / lax.psum(local_dot(direc, image), ("sub", "grp"))
+        alpha = rz_now / one_after_other(local_dot(direc, image), "sub", "grp")
         multipliers = multipliers + alpha * direc
         residual = residual - alpha * image
         if step + 1 < ITERS:

time: 929 us -> 1180 us (1.27)
  blocking collectives: 518 us -> 777 us
    psum x2 -> x6, blocking collectives: 214 us -> 480 us  [the longest x3 347 us: one_after_other(): inner = lax.psum(value_2, one)]
where the time goes in v1:
time: 1180 us
  blocking collectives  777 us (66%)
  waiting for transfers between devices  212 us (18%)
  matrix products  66.8 us (6%)
  other arithmetic  53 us (4%)
  starting transfers between devices  32.4 us (3%)
  local copies, waits for them, and re-layouts  22.8 us (2%)
  between operations  14.6 us (1%)
    psum x3, blocking collectives, one_after_other(): inner = lax.psum(value_2, one)  347 us
    psum x3, blocking collectives, norm_total(): return lax.psum(value, ('sub', 'grp'))  297 us
    psum x3, waiting for transfers between devices, local(): summed = lax.psum(primal, 'grp')  188 us
    psum x3, blocking collectives, one_after_other(): return lax.psum(inner, other)  133 us
    ppermute x6, starting transfers between devices, passed_along(): lax.ppermute(shard, axis, [(i, (i + by) % peers) for i in range(peers)])  31.9 us
    scatter-add x6, other arithmetic, local(): interior_load = zeros.at[rrow].add(apply_own).at[lrow].add(-apply_left)  24.6 us
  transfers between devices with their start and end apart: 9, of which 8 were waited for; matrix products, arithmetic and copies ran while one was open for 3% of the time, Pallas kernels for 0%

profile of v1, /device:TPU:1, one launch (start us, length us, event | category | flops | bytes accessed | tf_op | source)
XLA Modules:
  0.0 1178.2 jit_solution(6703106193194130141)
XLA Ops:
  9.1 4.4 collective-permute-start
  16.2 3.6 scatter_custom_fusion
  20.4 8.8 collective-permute-done
  29.9 4.7 scatter_custom_fusion.1
  34.7 2.5 fusion.46
  38.0 1.5 fusion.31
  40.3 1.5 fusion.13
  44.5 1.6 convolution_subtract_fusion.4
  46.2 2.7 convolution_bitcast_fusion.14
  49.2 2.7 convolution_bitcast_fusion.9
  51.8 67.6 %all-reduce.4.cloned.1.call-done = f32[128,256]{0,1:T(8,128)} async-done(((f32[128,256]{0,1:T(8,128)}), f32[128,256]{0,1:T(8,128)}) %all-reduce.4.cloned.1.call-update) | async-done | bytes 131088 | tf_op jit(solution)/shard_map/psum | solution.py:57
  120.6 3.3 fusion.2
  123.9 2.7 copy.17
  126.6 2.9 gather_fusion.1
  129.5 1.8 broadcast_select_fusion.2
  131.3 7.0 collective-permute-start.1
  139.7 2.9 gather_fusion
  142.6 1.9 multiply_reduce_fusion.2
  144.5 115.3 %psum.86 = f32[256]{0:T(256)} all-reduce(f32[256]{0:T(256)S(1)} %get-tuple-element.3), channel_id=1, replica_groups=mesh['sub'=64,'grp'=8] {'sub'}, use_global_device_ids=true, to_apply=%region_6.8 | all-reduce | flops 256 | bytes 2048 | tf_op jit(solution)/shard_map/psum | solution.py:11
  259.8 44.5 %psum.87 = f32[256]{0:T(256)} all-reduce(f32[256]{0:T(256)} %psum.86), channel_id=1, replica_groups=mesh['sub'=64,'grp'=8] {'grp'}, use_global_device_ids=true, to_apply=%region_7.9 | all-reduce | flops 256 | bytes 2048 | tf_op jit(solution)/shard_map/psum | solution.py:12
  304.4 98.7 %psum.84 = f32[256]{0:T(256)S(1)} all-reduce(f32[256]{0:T(256)} %get-tuple-element.4), channel_id=1, replica_groups=mesh['sub'=64,'grp'=8] {'sub','grp'}, use_global_device_ids=true, to_apply=%region_1.0 | all-reduce | flops 256 | bytes 2048 | tf_op jit(solution)/shard_map/psum | solution.py:21
  403.8 2.6 fusion.87
  406.3 99.6 %psum.88 = f32[256]{0:T(256)S(1)} all-reduce(f32[256]{0:T(256)} %get-tuple-element.7), channel_id=1, replica_groups=mesh['sub'=64,'grp'=8] {'sub','grp'}, use_global_device_ids=true, to_apply=%region_9.11 | all-reduce | flops 256 | bytes 2048 | tf_op jit(solution)/shard_map/psum | solution.py:21
  506.6 1.9 multiply_add_fusion.1
  508.4 2.7 collective-permute-start.2
  511.2 3.4 scatter_custom_fusion.2
  514.6 6.6 collective-permute-done.2
  521.1 4.9 scatter_custom_fusion.3
  526.0 3.3 fusion.43
  529.3 2.7 convolution_bitcast_fusion.13
  532.0 1.9 convolution_bitcast_fusion.8
  533.9 1.5 fusion.27
  536.2 1.5 fusion.9
  541.1 1.7 convolution_subtract_fusion.2
  543.1 2.6 convolution_bitcast_fusion.6
  545.7 61.3 %all-reduce.6.cloned.1.call-done = f32[128,256]{0,1:T(8,128)} async-done(((f32[128,256]{0,1:T(8,128)}), f32[128,256]{0,1:T(8,128)}) %all-reduce.6.cloned.1.call-update) | async-done | bytes 131088 | tf_op jit(solution)/shard_map/psum | solution.py:57
  608.2 3.4 fusion.1
  611.6 2.6 copy.19
  614.2 3.0 gather_fusion.3
  617.3 1.7 broadcast_select_fusion.1
  619.0 7.0 collective-permute-start.3
  626.0 3.1 gather_fusion.2
  629.6 1.8 multiply_reduce_fusion.1
  631.5 116.0 %psum.90 = f32[256]{0:T(256)} all-reduce(f32[256]{0:T(256)} %multiply_reduce_fusion.1), channel_id=1, replica_groups=mesh['sub'=64,'grp'=8] {'sub'}, use_global_device_ids=true, to_apply=%region_14.16 | all-reduce | flops 256 | bytes 2048 | tf_op jit(solution)/shard_map/psum | solution.py:11
  747.5 44.5 %psum.91 = f32[256]{0:T(256)} all-reduce(f32[256]{0:T(256)} %psum.90), channel_id=1, replica_groups=mesh['sub'=64,'grp'=8] {'grp'}, use_global_device_ids=true, to_apply=%region_15.17 | all-reduce | flops 256 | bytes 2048 | tf_op jit(solution)/shard_map/psum | solution.py:12
  793.3 2.6 fusion.88
  795.9 98.7 %psum.92 = f32[256]{0:T(256)} all-reduce(f32[256]{0:T(256)} %get-tuple-element.5), channel_id=1, replica_groups=mesh['sub'=64,'grp'=8] {'sub','grp'}, use_global_device_ids=true, to_apply=%region_17.19 | all-reduce | flops 256 | bytes 2048 | tf_op jit(solution)/shard_map/psum | solution.py:21
  895.2 1.8 multiply_add_fusion
  897.1 3.7 collective-permute-start.4
  900.7 3.4 scatter_custom_fusion.4
  904.1 5.4 collective-permute-done.4
  909.5 4.7 scatter_custom_fusion.5
  914.2 3.3 fusion.40
  917.5 2.7 convolution_bitcast_fusion.12
  920.2 1.9 convolution_bitcast_fusion.5
  929.3 1.7 convolution_subtract_fusion
  931.0 3.0 convolution_bitcast_fusion.3
  934.0 59.5 %all-reduce.8.cloned.1.call-done = f32[128,256]{0,1:T(8,128)} async-done(((f32[128,256]{0,1:T(8,128)}), f32[128,256]{0,1:T(8,128)}) %all-reduce.8.cloned.1.call-update) | async-done | bytes 131088 | tf_op jit(solution)/shard_map/psum | solution.py:57
  994.6 2.2 fusion
  998.5 7.1 collective-permute-start.5
  1006.8 2.2 collective-permute-done.5
  1010.1 115.5 %psum.94 = f32[256]{0:T(256)S(1)} all-reduce(f32[256]{0:T(256)S(1)} %multiply_reduce_fusion), channel_id=1, replica_groups=mesh['sub'=64,'grp'=8] {'sub'}, use_global_device_ids=true, to_apply=%region_22.24 | all-reduce | flops 256 | bytes 2048 | tf_op jit(solution)/shard_map/psum | solution.py:11
  1125.5 43.8 %psum.95 = f32[256]{0:T(256)S(1)} all-reduce(f32[256]{0:T(256)S(1)} %psum.94), channel_id=1, replica_groups=mesh['sub'=64,'grp'=8] {'grp'}, use_global_device_ids=true, to_apply=%region_23.25 | all-reduce | flops 256 | bytes 2048 | tf_op jit(solution)/shard_map/psum | solution.py:12
  1169.4 2.0 subtract_bitcast_fusion
  (116 shorter events, 34.7 us)
Async XLA Ops:
  7.2 39.0 %copy-start = (f32[1,1,3,384,128]{4,3,2,1,0:T(8,128)S(1)}, f32[1,1,3,384,128]{4,3,2,1,0:T(8,128)}, u32[]{:S(2)}) copy-start(f32[1,1,3,384,128]{4,3,2,1,0:T(8,128)} %param.18) | copy-start | bytes 1769476
  7.2 12.7 %copy-start.32 = (s32[1,1,256]{2,1,0:T(1,128)S(1)}, s32[1,1,256]{2,1,0:T(1,128)}, u32[]{:S(2)}) copy-start(s32[1,1,256]{2,1,0:T(1,128)} %param.15) | copy-start | bytes 3076
  7.2 112.2 %all-reduce.4.cloned.1.call-start = ((), (), s32[]{:S(2)}) async-start(), calls=%async_computation | async-start | bytes 262144 | tf_op jit(solution)/shard_map/psum | solution.py:57
  9.1 20.1 %collective-permute-start = (f32[256,256]{1,0:T(8,128)S(1)}, f32[256,256]{1,0:T(8,128)S(1)}, u32[]{:S(2)}, u32[]{:S(2)}) collective-permute-start(f32[256,256]{1,0:T(8,128)S(1)} %fusion.98), channel_id=1, source_target_pairs={{0,8},{8,16},{16,24},{24,32},{32,40},{40,48},{48,56},{56,64},{64,7... | collective-permute-start | bytes 786440 | tf_op jit(solution)/shard_map/ppermute | solution.py:17
  14.1 20.5 %copy-start.33 = (s32[256,1]{0,1:T(1,128)}, s32[256,1]{0,1:T(1,128)S(1)}, u32[]{:S(2)}) copy-start(s32[256,1]{0,1:T(1,128)S(1)} %compare_select_fusion) | copy-start | bytes 3076
  15.5 114.1 %copy-start.30 = (pred[256]{0:T(512)(128)(4,1)}, pred[256]{0:T(512)(128)(4,1)S(1)}, u32[]{:S(2)}) copy-start(pred[256]{0:T(512)(128)(4,1)S(1)} %compare_and_fusion) | copy-start | bytes 772
  16.2 13.0 %copy-start.34 = (s32[256,1]{0,1:T(1,128)}, s32[256,1]{0,1:T(1,128)S(1)}, u32[]{:S(2)}) copy-start(s32[256,1]{0,1:T(1,128)S(1)} %compare_select_fusion.1) | copy-start | bytes 3076
  16.2 110.4 %copy-start.22 = (s32[1024]{0:T(1024)}, s32[1024]{0:T(1024)S(1)}, u32[]{:S(2)}) copy-start(s32[1024]{0:T(1024)S(1)} %pad_clamp_fusion) | copy-start | bytes 12292
  16.2 18.4 %copy-start.1 = (f32[1,1,3,384,384]{4,3,2,1,0:T(8,128)S(1)}, f32[1,1,3,384,384]{4,3,2,1,0:T(8,128)}, u32[]{:S(2)}) copy-start(f32[1,1,3,384,384]{4,3,2,1,0:T(8,128)} %param.16) | copy-start | bytes 5308420
  29.2 0.7 copy-start.20
  29.9 7.3 copy-start.2
  34.6 3.4 copy-start.7
  42.7 1.8 copy-start.9
  44.5 1.7 copy-start.10
  48.9 558.1 %all-reduce.6.cloned.1.call-start = ((), (), s32[]{:S(2)}) async-start(), calls=%async_computation.1 | async-start | bytes 262144 | tf_op jit(solution)/shard_map/psum | solution.py:57
  131.3 11.3 collective-permute-start.1
  139.0 3.6 copy-start.23
  139.7 3.0 copy-start.21
  403.1 3.2 copy-start.25
  403.8 2.6 copy-start.26
  508.4 12.7 %collective-permute-start.2 = (f32[256,256]{1,0:T(8,128)}, f32[256,256]{1,0:T(8,128)}, u32[]{:S(2)}, u32[]{:S(2)}) collective-permute-start(f32[256,256]{1,0:T(8,128)} %multiply_add_fusion.1), channel_id=1, source_target_pairs={{0,8},{8,16},{16,24},{24,32},{32,40},{40,48},{48,56},{56,64},{64,7... | collective-permute-start | bytes 786440 | tf_op jit(solution)/shard_map/ppermute | solution.py:17
  526.0 3.3 copy-start.5
  532.0 1.9 copy-start.6
  538.5 1.8 copy-start.11
  538.6 2.6 copy-start.16
  540.4 0.7 copy-start.14
  542.8 450.6 %all-reduce.8.cloned.1.call-start = ((), (), s32[]{:S(2)}) async-start(), calls=%async_computation.2 | async-start | bytes 262144 | tf_op jit(solution)/shard_map/psum | solution.py:57
  619.0 10.6 collective-permute-start.3
  792.7 0.6 copy-start.28
  897.1 12.4 %collective-permute-start.4 = (f32[256,256]{1,0:T(8,128)}, f32[256,256]{1,0:T(8,128)}, u32[]{:S(2)}, u32[]{:S(2)}) collective-permute-start(f32[256,256]{1,0:T(8,128)} %multiply_add_fusion), channel_id=1, source_target_pairs={{0,8},{8,16},{16,24},{24,32},{32,40},{40,48},{48,56},{56,64},{64,7... | collective-permute-start | bytes 786440 | tf_op jit(solution)/shard_map/ppermute | solution.py:17
  914.2 3.3 copy-start.3
  920.2 1.9 copy-start.4
  926.7 1.8 copy-start.12
  926.7 2.6 copy-start.17
  928.6 0.7 copy-start.15
  931.0 62.5 %copy-start.19 = (f32[1,128,128]{2,1,0:T(8,128)S(1)}, f32[1,128,128]{2,1,0:T(8,128)}, u32[]{:S(2)}) copy-start(f32[1,128,128]{2,1,0:T(8,128)} %param.19) | copy-start | bytes 196612
  931.0 63.6 %copy-start.13 = (f32[256,384]{1,0:T(8,128)S(1)}, f32[256,384]{1,0:T(8,128)}, u32[]{:S(2)}) copy-start(f32[256,384]{1,0:T(8,128)} %copy-done.12) | copy-start | bytes 1179652
  997.2 1.1 copy-start.31
  998.5 170.9 %copy-start.24 = (f32[256]{0:T(256)S(1)}, f32[256]{0:T(256)}, u32[]{:S(2)}) copy-start(f32[256]{0:T(256)} %psum.92) | copy-start | bytes 3076
  998.5 170.9 %copy-start.8 = (f32[1,1,256,256]{3,2,1,0:T(8,128)S(1)}, f32[1,1,256,256]{3,2,1,0:T(8,128)}, u32[]{:S(2)}) copy-start(f32[1,1,256,256]{3,2,1,0:T(8,128)} %param.11) | copy-start | bytes 786436
  998.5 170.9 %copy-start.18 = (f32[256,256]{1,0:T(8,128)S(1)}, f32[256,256]{1,0:T(8,128)}, u32[]{:S(2)}) copy-start(f32[256,256]{1,0:T(8,128)} %get-tuple-element.6) | copy-start | bytes 786436
  998.5 170.9 %copy-start.27 = (f32[256]{0:T(256)S(1)}, f32[256]{0:T(256)}, u32[]{:S(2)}) copy-start(f32[256]{0:T(256)} %copy-done.26) | copy-start | bytes 3076
  998.5 170.9 %copy-start.29 = (f32[256]{0:T(256)S(1)}, f32[256]{0:T(256)}, u32[]{:S(2)}) copy-start(f32[256]{0:T(256)} %copy-done.28) | copy-start | bytes 3076
  998.5 10.4 collective-permute-start.5
Sparse Core Ops, SparseCore 0:
  49.0 70.3 all-reduce.3
  543.0 63.9 all-reduce.5
  931.1 62.2 all-reduce.7
